TPU v7x, 32 devices: a whole 2x2x4 slice. The times are simulated.
32 devices in a mesh: groups: 2 (over x), particle: 8 (over z, y), classes: 2 (over core).
Axes of the slice: x: 2, y: 2, z: 4, core: 2. Of those that a mesh axis runs over, the one named last changes fastest.
Arguments:
- boxes: bfloat16 [2048, 12288], P(('groups', 'particle', 'classes')), parts along dimension 0
- counts: int32 [32], P(('groups', 'particle', 'classes')), parts along dimension 0, may hold values from 1 to 64, as said below
- destinations: int32 [2048], P(('groups', 'particle', 'classes')), parts along dimension 0, may hold values from 0 to 7, as said below
- prior_rot: int32 [2048], P(('groups', 'particle', 'classes')), parts along dimension 0, may hold values from 0 to 23
- references: bfloat16 [128, 12288], P(('groups', 'classes')), parts along dimension 0
- cycle_weights: float32 [16, 64], P(('groups', 'particle')), parts along dimension 0, may hold values from 0.01 to 0.05
- prior_strength: float32 [128], P(('groups', 'classes')), parts along dimension 0, may hold values from 0.5 to 3
Outputs:
- new_references: float32 [128, 64, 192], P(('groups', 'classes'), 'particle'), parts along dimension 0
- log_evidence: float32 [2048], P(('groups', 'particle', 'classes')), parts along dimension 0
There are 2 independent parts, one for each index of `groups`. A program takes and returns all parts, laid end to end along the dimension named above; each array names one. Nothing has to cross between parts.
Inputs may be any that keep to these rules, and one draw needn't show every extreme that they name: On each index of classes, the counts of the 8 owners with that index sum to 128, and one of them is exactly 64. `destinations`: only an owner's first counts slots are picked; its other slots hold arbitrary indices. Each device receives exactly 16 picked boxes, all from owners with its own index of classes, and at most 8 from any one owner; some owner sends exactly 8 to one device.
All inputs are finite; a program needn't handle non-finite values.
Results may differ from a plain program's by a relative error of at most 0.004.
Values may be sent and summed in bfloat16 or wider, within the bound.
A program may use at most 192 MiB of HBM per device.

v0:
```python
import functools
import math

import jax
import jax.numpy as jnp
from jax import lax
from jax.experimental import pallas as pl
from jax.experimental.pallas import tpu as pltpu
from jax.sharding import PartitionSpec as P

CYCLES = 64
ANGLES = 192
ROTATIONS = 24
FINE = 4
COARSE = ROTATIONS // FINE
SHIFT = ANGLES // ROTATIONS
STEP_CYCLES = 4
STEP = STEP_CYCLES * ANGLES
STEPS = CYCLES // STEP_CYCLES
TWO_PI = 2.0 * math.pi


def roll_rows(block, shift):
    shift = shift % ANGLES
    if shift == 0:
        return block
    pieces = []
    for c in range(STEP_CYCLES):
        base = c * ANGLES
        pieces.append(block[base + ANGLES - shift : base + ANGLES])
        pieces.append(block[base : base + ANGLES - shift])
    return jnp.concatenate(pieces, axis=0)


def fan_out(rows, sign):
    plain = jnp.concatenate([rows, rows], axis=0).T
    low = lax.broadcasted_iota(jnp.int32, plain.shape, 1) < rows.shape[0]
    tiles = [
        jnp.where(low, roll_rows(plain, sign * SHIFT * f), roll_rows(plain, sign * SHIFT * (f + 1)))
        for f in range(0, FINE, 2)
    ]
    return jnp.concatenate([t.astype(jnp.bfloat16) for t in tiles], axis=1), plain


def kernel(cycles_dev, boxes_ref, refs_ref, wts_ref, aux_ref, str_ref, out_ref, ev_ref,
           acc, off, post, mass):
    phase, step = pl.program_id(0), pl.program_id(1)
    owned = boxes_ref.shape[0]
    half = str_ref.shape[1]

    @pl.when((phase == 0) & (step == 0))
    def _():
        acc[...] = jnp.zeros_like(acc)
        off[...] = jnp.zeros_like(off)

    @pl.when(phase == 0)
    def _():
        wts = wts_ref[0]
        lane = lax.broadcasted_iota(jnp.int32, (owned, STEP), 1)
        spread = jnp.broadcast_to(wts[:, 0:1], (owned, STEP))
        for c in range(1, STEP_CYCLES):
            spread = jnp.where(lane >= c * ANGLES, wts[:, c : c + 1], spread)
        scaled = boxes_ref[...].astype(jnp.float32) * spread
        high = scaled.astype(jnp.bfloat16)
        rest = (scaled - high.astype(jnp.float32)).astype(jnp.bfloat16)
        lhs = jnp.concatenate([high, rest], axis=0)
        fan, plain = fan_out(refs_ref[...].astype(jnp.float32), 1)
        total = off[...]
        for c in range(STEP_CYCLES):
            piece = plain[c * ANGLES : (c + 1) * ANGLES]
            total = total + wts[:, c : c + 1] * jnp.sum(piece * piece, axis=0, keepdims=True)
        off[...] = total
        for q in range(COARSE):
            acc[q] += jnp.dot(
                lhs, roll_rows(fan, SHIFT * FINE * q), preferred_element_type=jnp.float32
            )

    @pl.when((phase == 0) & (step == STEPS - 1))
    def _():
        aux = aux_ref[...]
        live = aux[:, ROTATIONS : ROTATIONS + 1]
        wsum = aux[:, ROTATIONS + 1 : ROTATIONS + 2]
        low = lax.broadcasted_iota(jnp.int32, (owned, half), 1) < owned
        base = -0.5 * off[...]
        strength = str_ref[...]
        top = None
        for q in range(COARSE):
            for t in range(FINE // 2):
                r = q * FINE + 2 * t
                cols = slice(t * half, (t + 1) * half)
                turn = jnp.where(low, aux[:, r : r + 1], aux[:, r + 1 : r + 2])
                score = acc[q, :owned, cols] + acc[q, owned:, cols] + base + turn * strength
                acc[q, :owned, cols] = score
                top = score if top is None else jnp.maximum(top, score)
        top = jnp.max(top, axis=1, keepdims=True)
        norm = jnp.zeros((owned, half), jnp.float32)
        for q in range(COARSE):
            for t in range(FINE // 2):
                cols = slice(t * half, (t + 1) * half)
                term = jnp.exp(acc[q, :owned, cols] - top)
                acc[q, :owned, cols] = term
                norm = norm + term
        norm = jnp.sum(norm, axis=1, keepdims=True)
        ev_ref[...] = jnp.where(live > 0.0, (top + jnp.log(norm)) / (ANGLES * wsum), 0.0)
        seen = jnp.zeros((owned, half), jnp.float32)

        def weight(q, t):
            cols = slice(t * half, (t + 1) * half)
            value = jnp.where(live > 0.0, acc[q, :owned, cols] / norm, 0.0)
            return value.astype(jnp.bfloat16).astype(jnp.float32)

        for q in range(0, COARSE, 2):
            for t in range(FINE // 2):
                first, second = weight(q, t), weight(q + 1, t)
                seen = seen + first + second
                even = jnp.where(low, first, pltpu.roll(second, half // 2, 1))
                odd = jnp.where(low, pltpu.roll(first, half // 2, 1), second)
                cols = slice(q // 2 * half, (q // 2 + 1) * half)
                post[2 * t * owned : (2 * t + 1) * owned, cols] = even.astype(jnp.bfloat16)
                post[(2 * t + 1) * owned : (2 * t + 2) * owned, cols] = odd.astype(jnp.bfloat16)
        seen = jnp.sum(seen, axis=0, keepdims=True)
        seen = jnp.broadcast_to(seen, (half, half))
        seen = seen + pltpu.roll(seen, half // 2, 1)
        mass[...] = seen.T

    @pl.when(phase == 1)
    def _():
        fan, _unused = fan_out(boxes_ref[...].astype(jnp.float32), -1)
        sums = jnp.dot(fan, post[...], preferred_element_type=jnp.float32)
        both = sums[:, :half]
        for p in range(1, COARSE // 2):
            both = both + roll_rows(sums[:, p * half : (p + 1) * half], -2 * p * SHIFT * FINE)
        whole = both + pltpu.roll(roll_rows(both, -SHIFT * FINE), half // 2, 1)
        turned = whole.T
        classes = half // 4
        width = cycles_dev * ANGLES
        for h in range(2):
            rows = turned[h * classes : (h + 1) * classes]
            tail = mass[h * classes : (h + 1) * classes, :]
            if width >= STEP:
                start = pl.multiple_of(step % (width // STEP) * STEP, 128)
                out_ref[0, h, :, pl.ds(start, STEP)] = rows
                out_ref[0, h, :, width:] = tail[:, : out_ref.shape[3] - width]
            else:
                for j in range(STEP // width):
                    out_ref[j, h, :, :width] = rows[:, j * width : (j + 1) * width]
                    out_ref[j, h, :, width:] = tail[:, : out_ref.shape[3] - width]


def class_terms(boxes, refs, wts, aux, strength, peers):
    cycles_dev = CYCLES // peers
    width = cycles_dev * ANGLES
    padded = (width + 1 + 127) // 128 * 128
    owned = boxes.shape[0]
    classes = refs.shape[0]
    half = 2 * classes
    if width >= STEP:
        per = width // STEP
        out_spec = pl.BlockSpec((1, 2, classes // 2, padded), lambda p, i: (p * (i // per), 0, 0, 0))
    else:
        out_spec = pl.BlockSpec(
            (STEP // width, 2, classes // 2, padded), lambda p, i: (p * i, 0, 0, 0)
        )
    hold = lambda p, i: i * (1 - p) + (STEPS - 1) * p
    return pl.pallas_call(
        functools.partial(kernel, cycles_dev),
        grid=(2, STEPS),
        in_specs=[
            pl.BlockSpec((owned, STEP), lambda p, i: (0, i)),
            pl.BlockSpec((classes, STEP), lambda p, i: (0, hold(p, i))),
            pl.BlockSpec((1, owned, STEP_CYCLES), lambda p, i: (hold(p, i), 0, 0)),
            pl.BlockSpec(aux.shape, lambda p, i: (0, 0)),
            pl.BlockSpec((1, half), lambda p, i: (0, 0)),
        ],
        out_specs=[out_spec, pl.BlockSpec((owned, 1), lambda p, i: (0, 0))],
        out_shape=[
            jax.ShapeDtypeStruct((peers, 2, classes // 2, padded), jnp.float32),
            jax.ShapeDtypeStruct((owned, 1), jnp.float32),
        ],
        scratch_shapes=[
            pltpu.VMEM((COARSE, 2 * owned, FINE * classes), jnp.float32),
            pltpu.VMEM((owned, half), jnp.float32),
            pltpu.VMEM((FINE * owned, COARSE * classes), jnp.bfloat16),
            pltpu.VMEM((half, half), jnp.float32),
        ],
        compiler_params=pltpu.CompilerParams(
            dimension_semantics=("arbitrary", "arbitrary"), vmem_limit_bytes=40 * 1024 * 1024
        ),
    )(boxes, refs, wts, aux, strength)


def on_device(boxes, counts, destinations, prior_rot, references, cycle_weights, prior_strength):
    peers = lax.axis_size("particle")
    cycle_index = lax.axis_index("particle")
    cycles_dev = CYCLES // peers
    width = cycles_dev * ANGLES
    owned = boxes.shape[0]
    refs = lax.all_gather(references, "classes", axis=0, tiled=True)
    small = lax.all_gather(
        jnp.concatenate([cycle_weights[0], prior_strength]), ("particle", "classes"), axis=0
    )
    small = small.reshape(peers, 2, -1)
    group_wts = small[:, 0, :CYCLES]
    strength = small[0, :, CYCLES:].reshape(1, -1)
    mine = destinations[:, None] == jnp.arange(peers, dtype=jnp.int32)[None, :]
    wts = jnp.sum(jnp.where(mine[:, :, None], group_wts[None], 0.0), axis=1)
    live = (jnp.arange(owned, dtype=jnp.int32) < counts[0]).astype(jnp.float32)
    turn_ids = jnp.arange(ROTATIONS, dtype=jnp.float32)
    gap = TWO_PI * (turn_ids[None, :] - prior_rot[:, None].astype(jnp.float32)) / ROTATIONS
    aux = jnp.concatenate([jnp.cos(gap), live[:, None], jnp.sum(wts, axis=1)[:, None]], axis=1)
    wts = jnp.transpose(wts.reshape(owned, STEPS, STEP_CYCLES), (1, 0, 2))
    parts, evidence = class_terms(
        boxes, refs, wts, aux, jnp.concatenate([strength, strength], axis=1), peers
    )
    classes_dev = references.shape[0]
    sums = lax.psum_scatter(
        parts.reshape(peers * 2, classes_dev, -1), ("particle", "classes"), scatter_dimension=0
    )
    own_refs = lax.dynamic_slice_in_dim(references, cycle_index * width, width, 1)
    new_references = (sums[:, :width] + own_refs.astype(jnp.float32)) / (
        sums[:, width : width + 1] + 1.0
    )
    return new_references.reshape(classes_dev, cycles_dev, ANGLES), evidence[:, 0]


def solution(mesh):
    in_specs = (
        P(("groups", "particle", "classes"), None),
        P(("groups", "particle", "classes")),
        P(("groups", "particle", "classes")),
        P(("groups", "particle", "classes")),
        P(("groups", "classes"), None),
        P(("groups", "particle"), None),
        P(("groups", "classes")),
    )
    out_specs = (P(("groups", "classes"), "particle", None), P(("groups", "particle", "classes")))
    return jax.shard_map(
        on_device, mesh=mesh, in_specs=in_specs, out_specs=out_specs, check_vma=False
    )
```

profile of v0, /device:TPU:0, one launch (start us, length us, event | category | flops | bytes accessed | tf_op | source)
XLA Modules:
  0.0 150.2 jit_solution(13644377068312955139)
XLA Ops:
  7.2 0.7 all-gather.3.cloned.1.call-update
  7.9 0.0 reduce-scatter.2.cloned.1.call-start
  8.0 1.2 dynamic-slice
  9.9 0.9 maximum_dynamic-update-slice_fusion
  10.7 35.4 %all-reduce = f32[1536]{0:T(1024)S(1)} all-reduce(f32[1536]{0:T(1024)S(1)} %maximum_dynamic-update-slice_fusion), channel_id=2, replica_groups=mesh['groups'=2,'particle'=8,'classes'=2] {'particle','classes'}, use_global_device_ids=true, to_apply=%add | all-reduce | flops 1536 | bytes 12288
  46.2 0.1 reshape.50
  46.2 0.1 slice.17
  47.0 0.7 convert_element_type.17
  47.6 0.1 reshape_squeeze.3
  47.7 0.7 iota_compare_fusion.1
  48.4 0.9 select_reduce_fusion
  49.4 0.1 copy.14
  49.5 0.1 copy.12
  49.6 0.3 copy.13
  49.8 0.1 pad_maximum_fusion.1.str_ref
  49.9 0.2 multiply_cosine_fusion
  50.1 0.1 pad_maximum_fusion.aux_ref
  50.2 1.4 copy-done.1
  51.6 24.3 %shard_map.86 = (f32[8,2,32,1664]{3,2,1,0:T(8,128)}, f32[64,1]{1,0:T(8,128)S(1)}) custom-call(bf16[64,12288]{1,0:T(8,128)(2,1)S(1)} %copy-done, bf16[64,12288]{1,0:T(8,128)(2,1)S(1)} %copy-done.1, f32[16,64,4]{2,1,0:T(8,128)S(1)} %bitcast.10, f32[64,26]{1,0:T(8,128)S(1)} %pad_maximum_fusion.aux_ref, f32[1,128]{1,0:T(1,128)S(1)} %pad_maximum_fusion.1.str_ref), custom_call_target="tpu_custom_call" | custom-call | tf_op jit(solution)/shard_map/pallas_call | solution.py:165
  76.0 0.6 reduce.2
  76.6 64.0 %reduce-scatter.2.cloned.1.call-done = f32[1,32,1664]{2,1,0:T(8,128)} async-done(((f32[16,32,1664]{2,1,0:T(8,128)}), f32[1,32,1664]{2,1,0:T(8,128)}) %reduce-scatter.2.cloned.1.call-update) | async-done | bytes 213008 | tf_op jit(solution)/shard_map/reduce_scatter | solution.py:216
  140.6 0.8 fusion.2
  141.4 1.1 fusion
  142.5 0.8 reshape.53
  (9 shorter events, 0.1 us)
Async XLA Ops:
  7.2 43.1 %copy-start = (bf16[64,12288]{1,0:T(8,128)(2,1)S(1)}, bf16[64,12288]{1,0:T(8,128)(2,1)}, u32[]{:S(2)}) copy-start(bf16[64,12288]{1,0:T(8,128)(2,1)} %boxes_ref.1) | copy-start | bytes 4718596
  7.2 43.0 %all-gather.3.cloned.1.call-start = ((), (), s32[]{:S(2)}) async-start(), calls=%async_computation.1 | async-start | bytes 2359296 | tf_op jit(solution)/shard_map/all_gather | solution.py:198
  7.9 132.7 %reduce-scatter.2.cloned.1.call-start = ((), (), s32[]{:S(2)}) async-start(), calls=%async_computation.2 | async-start | bytes 3620864 | tf_op jit(solution)/shard_map/reduce_scatter | solution.py:216
  50.2 1.4 copy-start.1
Sparse Core Ops, SparseCore 0:
  9.5 12.5 all-gather.2
  76.1 64.4 reduce-scatter.1
where the time goes:
time: 150 us
  waiting for transfers between devices  64.7 us (43%)
  blocking collectives  35.4 us (24%)
  Pallas kernels  24.3 us (16%)
  between operations  15.4 us (10%)
  other arithmetic  6.09 us (4%)
  local copies, waits for them, and re-layouts  4.12 us (3%)
    reduce_scatter x1, waiting for transfers between devices, on_device(): lax.psum_scatter(parts.reshape(peers * 2, classes_dev, -1), ('particle',...  64 us
    unnamed x1, blocking collectives  35.4 us
    pallas_call x1, Pallas kernels, class_terms(): pl.pallas_call(functools.partial(kernel, cycles_dev), grid=(2, STEPS), in...  24.3 us
  transfers between devices with their start and end apart: 2, of which 1 were waited for; matrix products, arithmetic and copies ran while one was open for 4% of the time, Pallas kernels for 0%

commit v1 on v0

--- a/solution.py
+++ b/solution.py
@@ -189,19 +189,164 @@
     )(boxes, refs, wts, aux, strength)
 
 
+MESH = pl.DeviceIdType.MESH
+CHUNKS = 4
+
+
+def greet(devices):
+    barrier = pltpu.get_barrier_semaphore()
+    for device in devices:
+        pl.semaphore_signal(barrier, inc=1, device_id=device, device_id_type=MESH)
+    pl.semaphore_wait(barrier, len(devices))
+
+
+def gather_kernel(peers, refs_ref, row_ref, all_refs, all_rows, local, send, recv):
+    mine, core = lax.axis_index("particle"), lax.axis_index("classes")
+    partner = {"classes": 1 - core}
+    others = [{"particle": lax.rem(mine + d, peers)} for d in range(1, peers)]
+    greet([partner] + others)
+    copies = [
+        pltpu.make_async_remote_copy(
+            src_ref=refs_ref, dst_ref=all_refs.at[core], send_sem=send.at[0], recv_sem=recv.at[0],
+            device_id=partner, device_id_type=MESH,
+        ),
+        pltpu.make_async_remote_copy(
+            src_ref=row_ref, dst_ref=all_rows.at[peers], send_sem=send.at[1], recv_sem=recv.at[1],
+            device_id=partner, device_id_type=MESH,
+        ),
+    ]
+    for d, other in enumerate(others):
+        copies.append(
+            pltpu.make_async_remote_copy(
+                src_ref=row_ref, dst_ref=all_rows.at[mine], send_sem=send.at[2 + d],
+                recv_sem=recv.at[2 + d], device_id=other, device_id_type=MESH,
+            )
+        )
+    for copy in copies:
+        copy.start()
+    own = [
+        pltpu.make_async_copy(refs_ref, all_refs.at[core], local.at[0]),
+        pltpu.make_async_copy(row_ref, all_rows.at[mine], local.at[1]),
+    ]
+    for copy in own:
+        copy.start()
+    for copy in own + copies:
+        copy.wait()
+
+
+def gathered(refs, row, peers):
+    return pl.pallas_call(
+        functools.partial(gather_kernel, peers),
+        in_specs=[pl.BlockSpec(memory_space=pltpu.VMEM)] * 2,
+        out_specs=[pl.BlockSpec(memory_space=pltpu.VMEM)] * 2,
+        out_shape=[
+            jax.ShapeDtypeStruct((2,) + refs.shape, refs.dtype),
+            jax.ShapeDtypeStruct((peers + 1,) + row.shape, row.dtype),
+        ],
+        scratch_shapes=[
+            pltpu.SemaphoreType.DMA((2,)),
+            pltpu.SemaphoreType.DMA((peers + 1,)),
+            pltpu.SemaphoreType.DMA((peers + 1,)),
+        ],
+        compiler_params=pltpu.CompilerParams(collective_id=0, has_side_effects=True),
+    )(refs, row)
+
+
+def scatter_kernel(depth, parts, out, pair_in, side_out, side_in, line_out, line_in,
+                   pair_send, pair_recv, side_send, side_recv, line_send, line_recv):
+    mine, core = lax.axis_index("particle"), lax.axis_index("classes")
+    level, side = mine // 2, lax.rem(mine, 2)
+    partner = {"classes": 1 - core}
+    across = {"particle": level * 2 + 1 - side}
+    levels = [lax.rem(level + d, depth) for d in range(1, depth)]
+    line = [{"particle": other * 2 + side} for other in levels]
+    greet([partner, across] + line)
+    rows = out.shape[0] // CHUNKS
+    pair, cross, lines = [], [], []
+    for j in range(CHUNKS):
+        copy = pltpu.make_async_remote_copy(
+            src_ref=parts.at[:, :, 1 - core, j * rows : (j + 1) * rows], dst_ref=pair_in.at[j],
+            send_sem=pair_send.at[j], recv_sem=pair_recv.at[j], device_id=partner,
+            device_id_type=MESH,
+        )
+        copy.start()
+        pair.append(copy)
+    for j in range(CHUNKS):
+        span = slice(j * rows, (j + 1) * rows)
+        pair[j].wait_recv()
+        side_out[j] = parts[:, 1 - side, core, span] + pair_in[j, :, 1 - side]
+        copy = pltpu.make_async_remote_copy(
+            src_ref=side_out.at[j], dst_ref=side_in.at[j], send_sem=side_send.at[j],
+            recv_sem=side_recv.at[j], device_id=across, device_id_type=MESH,
+        )
+        copy.start()
+        cross.append(copy)
+        line_out[j] = parts[:, side, core, span] + pair_in[j, :, side]
+    for j in range(CHUNKS):
+        cross[j].wait_recv()
+        line_out[j] = line_out[j] + side_in[j]
+        for d in range(depth - 1):
+            copy = pltpu.make_async_remote_copy(
+                src_ref=line_out.at[j, levels[d]], dst_ref=line_in.at[j, d],
+                send_sem=line_send.at[j, d], recv_sem=line_recv.at[j, d], device_id=line[d],
+                device_id_type=MESH,
+            )
+            copy.start()
+            lines.append(copy)
+    for j in range(CHUNKS):
+        total = line_out[j, level]
+        for d in range(depth - 1):
+            lines[j * (depth - 1) + d].wait_recv()
+            total = total + line_in[j, d]
+        out[j * rows : (j + 1) * rows] = total
+    for copy in pair + cross + lines:
+        copy.wait_send()
+
+
+def scattered(parts):
+    peers, _, classes, width = parts.shape
+    depth = peers // 2
+    rows = classes // CHUNKS
+    sems = pltpu.SemaphoreType.DMA((CHUNKS,))
+    line_sems = pltpu.SemaphoreType.DMA((CHUNKS, max(depth - 1, 1)))
+    return pl.pallas_call(
+        functools.partial(scatter_kernel, depth),
+        in_specs=[pl.BlockSpec(memory_space=pltpu.VMEM)],
+        out_specs=pl.BlockSpec(memory_space=pltpu.VMEM),
+        out_shape=jax.ShapeDtypeStruct((classes, width), jnp.float32),
+        scratch_shapes=[
+            pltpu.VMEM((CHUNKS, depth, 2, rows, width), jnp.float32),
+            pltpu.VMEM((CHUNKS, depth, rows, width), jnp.float32),
+            pltpu.VMEM((CHUNKS, depth, rows, width), jnp.float32),
+            pltpu.VMEM((CHUNKS, depth, rows, width), jnp.float32),
+            pltpu.VMEM((CHUNKS, max(depth - 1, 1), rows, width), jnp.float32),
+            sems, sems, sems, sems, line_sems, line_sems,
+        ],
+        compiler_params=pltpu.CompilerParams(
+            collective_id=1, has_side_effects=True, vmem_limit_bytes=48 * 1024 * 1024
+        ),
+    )(parts.reshape(depth, 2, 2, classes, width))
+
+
 def on_device(boxes, counts, destinations, prior_rot, references, cycle_weights, prior_strength):
     peers = lax.axis_size("particle")
     cycle_index = lax.axis_index("particle")
     cycles_dev = CYCLES // peers
     width = cycles_dev * ANGLES
     owned = boxes.shape[0]
-    refs = lax.all_gather(references, "classes", axis=0, tiled=True)
-    small = lax.all_gather(
-        jnp.concatenate([cycle_weights[0], prior_strength]), ("particle", "classes"), axis=0
-    )
-    small = small.reshape(peers, 2, -1)
-    group_wts = small[:, 0, :CYCLES]
-    strength = small[0, :, CYCLES:].reshape(1, -1)
+    classes_dev = references.shape[0]
+    lane_index = lax.axis_index("classes")
+    row = jnp.concatenate([cycle_weights[0], prior_strength])
+    row = jnp.pad(row, (0, 128 - row.shape[0]))[None, :]
+    refs, rows = gathered(references, row, peers)
+    refs = refs.reshape(2 * classes_dev, -1)
+    group_wts = rows[:peers, 0, :CYCLES]
+    other = rows[peers, 0, CYCLES : CYCLES + classes_dev]
+    strength = jnp.where(
+        lane_index == 0,
+        jnp.concatenate([prior_strength, other]),
+        jnp.concatenate([other, prior_strength]),
+    ).reshape(1, -1)
     mine = destinations[:, None] == jnp.arange(peers, dtype=jnp.int32)[None, :]
     wts = jnp.sum(jnp.where(mine[:, :, None], group_wts[None], 0.0), axis=1)
     live = (jnp.arange(owned, dtype=jnp.int32) < counts[0]).astype(jnp.float32)
@@ -212,10 +357,7 @@
     parts, evidence = class_terms(
         boxes, refs, wts, aux, jnp.concatenate([strength, strength], axis=1), peers
     )
-    classes_dev = references.shape[0]
-    sums = lax.psum_scatter(
-        parts.reshape(peers * 2, classes_dev, -1), ("particle", "classes"), scatter_dimension=0
-    )
+    sums = scattered(parts)
     own_refs = lax.dynamic_slice_in_dim(references, cycle_index * width, width, 1)
     new_references = (sums[:, :width] + own_refs.astype(jnp.float32)) / (
         sums[:, width : width + 1] + 1.0

time: 150 us -> 75.4 us (0.50)
  waiting for transfers between devices: 64.7 us -> 0 us
  Pallas kernels: 24.3 us -> 63.1 us
  blocking collectives: 35.4 us -> 0 us
  between operations: 15.4 us -> 1.49 us
    reduce_scatter x1 -> x0, waiting for transfers between devices: 64 us -> none  [on_device(): lax.psum_scatter(parts.reshape(peers * 2, classes_dev, -1), ('particle',...]
    pallas_call x0 -> x2, Pallas kernels: none -> 40.4 us  [the longest x1 29.8 us: scattered(): pl.pallas_call(functools.partial(scatter_kernel, depth), in_specs=[pl.Blo...]
    unnamed x1 -> x0, blocking collectives: 35.4 us -> none
    pallas_call x1, Pallas kernels: 24.3 us -> 22.7 us  [class_terms(): pl.pallas_call(functools.partial(kernel, cycles_dev), grid=(2, STEPS), in...]
  transfers between devices with their start and end apart: 2 -> 0, of which waited for: 1 -> 0; matrix products, arithmetic and copies ran while one was open for 4% -> 0% of each run, Pallas kernels for 0% -> 0%
where the time goes in v1:
time: 75.4 us; the launch traced here: 75.1 us
  Pallas kernels  63.1 us (84%)
  other arithmetic  6.48 us (9%)
  local copies, waits for them, and re-layouts  4.04 us (5%)
  between operations  1.49 us (2%)
    pallas_call x1, Pallas kernels, scattered(): pl.pallas_call(functools.partial(scatter_kernel, depth), in_specs=[pl.Blo...  29.8 us
    pallas_call x1, Pallas kernels, class_terms(): pl.pallas_call(functools.partial(kernel, cycles_dev), grid=(2, STEPS), in...  22.7 us
    pallas_call x1, Pallas kernels, gathered(): pl.pallas_call(functools.partial(gather_kernel, peers), in_specs=[pl.Bloc...  10.6 us

profile of v1, /device:TPU:0, one launch (start us, length us, event | category | flops | bytes accessed | tf_op | source)
XLA Modules:
  0.0 75.1 jit_solution(9771311261641341276)
XLA Ops:
  0.6 0.0 copy-start
  1.4 0.7 convert_element_type.19
  2.1 1.3 %fusion.2.row_ref = f32[1,128]{1,0:T(1,128)} fusion(f32[32]{0:T(128)} %param.13, f32[64]{0:T(128)} %bitcast.21), kind=kLoop, calls=%fused_computation.15 | loop fusion | flops 512 | bytes 896 | tf_op jit(solution)/shard_map/broadcast_in_dim | solution.py:340
  3.3 0.7 iota_compare_fusion.1
  4.1 0.2 multiply_cosine_fusion
  4.3 10.6 %shard_map.86 = (bf16[2,32,12288]{2,1,0:T(8,128)(2,1)}, f32[9,1,128]{2,1,0:T(1,128)}) custom-call(bf16[32,12288]{1,0:T(8,128)(2,1)} %refs_ref.1, f32[1,128]{1,0:T(1,128)} %fusion.2.row_ref), custom_call_target="tpu_custom_call" | custom-call | tf_op jit(solution)/shard_map/pallas_call | solution.py:238
  14.9 0.7 slice_bitcast_fusion
  15.6 0.7 slice.12
  16.3 0.8 %broadcast_select_fusion = f32[1,64]{1,0:T(1,128)S(1)} fusion(pred[]{:T(512)S(6)} %eq.23, f32[1,32]{1,0:T(1,128)S(1)} %slice_bitcast_fusion, f32[1,32]{1,0:T(1,128)} %bitcast.20), kind=kLoop, calls=%fused_computation.11 | loop fusion | flops 192 | bytes 513 | tf_op jit(solution)/shard_map/jit(_where)/select_n | solution.py:345
  17.1 0.1 pad_maximum_fusion.1.str_ref
  17.2 0.9 %select_reduce_fusion = (f32[64]{0:T(128)S(1)}, f32[64,64]{1,0:T(8,128)S(1)}) fusion(f32[8,64]{1,0:T(8,128)S(1)} %bitcast.18, pred[64,8]{1,0:T(8,128)(4,1)S(1)} %iota_compare_fusion.1), kind=kLoop, calls=%fused_computation | loop fusion | flops 94144 | bytes 19200 | tf_op jit(solution)/shard_map/reduce_sum | solution.py:355
  18.1 0.1 copy.14
  18.2 0.1 pad_maximum_fusion.aux_ref
  18.3 0.1 copy.12
  18.4 0.2 copy.13
  18.6 0.0 copy-done
  18.7 0.0 copy-start.1
  18.7 1.4 %copy-done.1 = bf16[2,32,12288]{2,1,0:T(8,128)(2,1)S(1)} copy-done((bf16[2,32,12288]{2,1,0:T(8,128)(2,1)S(1)}, bf16[2,32,12288]{2,1,0:T(8,128)(2,1)}, u32[]{:S(2)}) %copy-start.1) | copy-done | bytes 1572888
  20.1 22.7 %shard_map.87 = (f32[8,2,32,1664]{3,2,1,0:T(8,128)S(1)}, f32[64,1]{1,0:T(8,128)S(1)}) custom-call(bf16[64,12288]{1,0:T(8,128)(2,1)S(1)} %copy-done, bf16[64,12288]{1,0:T(8,128)(2,1)S(1)} %bitcast.16, f32[16,64,4]{2,1,0:T(8,128)S(1)} %bitcast.15, f32[64,26]{1,0:T(8,128)S(1)} %pad_maximum_fusion.aux_ref, f32[1,128]{1,0:T(1,128)S(1)} %pad_maximum_fusion.1.str_ref), custom_call_target="tpu_custom_call" | custom-call | tf_op jit(solution)/shard_map/pallas_call | solution.py:165
  42.8 29.8 %shard_map.88 = f32[32,1664]{1,0:T(8,128)S(1)} custom-call(f32[4,2,2,32,1664]{4,3,2,1,0:T(8,128)S(1)} %bitcast.14), custom_call_target="tpu_custom_call" | custom-call | tf_op jit(solution)/shard_map/pallas_call | solution.py:312
  72.6 0.1 add_reduce_fusion
  72.7 1.0 %add_divide_fusion = f32[32,1536]{1,0:T(8,128)S(1)} fusion(f32[32,1664]{1,0:T(8,128)S(1)} %shard_map.88, f32[32]{0:T(128)S(1)} %add_reduce_fusion, bf16[32,12288]{1,0:T(8,128)(2,1)} %refs_ref.1, s32[]{:T(128)S(6)} %select_n.25), kind=kLoop, calls=%fused_computation.2 | loop fusion | flops 147456 | bytes 491652 | tf_op jit(solution)/shard_map/div | solution.py:362
  73.7 0.6 reduce.2
  74.3 0.8 %reshape.111 = f32[32,8,192]{2,1,0:T(8,128)} reshape(f32[32,1536]{1,0:T(8,128)S(1)} %add_divide_fusion) | data formatting | bytes 393216 | tf_op jit(solution)/shard_map/reshape | solution.py:365
  (1 shorter events, 0.0 us)
Async XLA Ops:
  0.6 18.0 %copy-start = (bf16[64,12288]{1,0:T(8,128)(2,1)S(1)}, bf16[64,12288]{1,0:T(8,128)(2,1)}, u32[]{:S(2)}) copy-start(bf16[64,12288]{1,0:T(8,128)(2,1)} %boxes_ref.1) | copy-start | bytes 4718596
  18.7 1.4 %copy-start.1 = (bf16[2,32,12288]{2,1,0:T(8,128)(2,1)S(1)}, bf16[2,32,12288]{2,1,0:T(8,128)(2,1)}, u32[]{:S(2)}) copy-start(bf16[2,32,12288]{2,1,0:T(8,128)(2,1)} %get-tuple-element.6) | copy-start | bytes 4718596

commit v2 on v1

--- a/solution.py
+++ b/solution.py
@@ -42,18 +42,17 @@
     return jnp.concatenate([t.astype(jnp.bfloat16) for t in tiles], axis=1), plain
 
 
-def kernel(cycles_dev, boxes_ref, refs_ref, wts_ref, aux_ref, str_ref, out_ref, ev_ref,
-           acc, off, post, mass):
-    phase, step = pl.program_id(0), pl.program_id(1)
+def score_kernel(boxes_ref, refs_ref, wts_ref, aux_ref, str_ref, post, mass, ev_ref, acc, off):
+    step = pl.program_id(0)
     owned = boxes_ref.shape[0]
     half = str_ref.shape[1]
 
-    @pl.when((phase == 0) & (step == 0))
+    @pl.when(step == 0)
     def _():
         acc[...] = jnp.zeros_like(acc)
         off[...] = jnp.zeros_like(off)
 
-    @pl.when(phase == 0)
+    @pl.when(step >= 0)
     def _():
         wts = wts_ref[0]
         lane = lax.broadcasted_iota(jnp.int32, (owned, STEP), 1)
@@ -75,7 +74,7 @@
                 lhs, roll_rows(fan, SHIFT * FINE * q), preferred_element_type=jnp.float32
             )
 
-    @pl.when((phase == 0) & (step == STEPS - 1))
+    @pl.when(step == STEPS - 1)
     def _():
         aux = aux_ref[...]
         live = aux[:, ROTATIONS : ROTATIONS + 1]
@@ -119,72 +118,74 @@
                 post[2 * t * owned : (2 * t + 1) * owned, cols] = even.astype(jnp.bfloat16)
                 post[(2 * t + 1) * owned : (2 * t + 2) * owned, cols] = odd.astype(jnp.bfloat16)
         seen = jnp.sum(seen, axis=0, keepdims=True)
-        seen = jnp.broadcast_to(seen, (half, half))
-        seen = seen + pltpu.roll(seen, half // 2, 1)
-        mass[...] = seen.T
-
-    @pl.when(phase == 1)
-    def _():
-        fan, _unused = fan_out(boxes_ref[...].astype(jnp.float32), -1)
-        sums = jnp.dot(fan, post[...], preferred_element_type=jnp.float32)
-        both = sums[:, :half]
-        for p in range(1, COARSE // 2):
-            both = both + roll_rows(sums[:, p * half : (p + 1) * half], -2 * p * SHIFT * FINE)
-        whole = both + pltpu.roll(roll_rows(both, -SHIFT * FINE), half // 2, 1)
-        turned = whole.T
-        classes = half // 4
-        width = cycles_dev * ANGLES
-        for h in range(2):
-            rows = turned[h * classes : (h + 1) * classes]
-            tail = mass[h * classes : (h + 1) * classes, :]
-            if width >= STEP:
-                start = pl.multiple_of(step % (width // STEP) * STEP, 128)
-                out_ref[0, h, :, pl.ds(start, STEP)] = rows
-                out_ref[0, h, :, width:] = tail[:, : out_ref.shape[3] - width]
-            else:
-                for j in range(STEP // width):
-                    out_ref[j, h, :, :width] = rows[:, j * width : (j + 1) * width]
-                    out_ref[j, h, :, width:] = tail[:, : out_ref.shape[3] - width]
-
-
-def class_terms(boxes, refs, wts, aux, strength, peers):
-    cycles_dev = CYCLES // peers
-    width = cycles_dev * ANGLES
+        mass[...] = seen + pltpu.roll(seen, half // 2, 1)
+
+
+def turned_sums(boxes, post):
+    half = 2 * boxes.shape[0]
+    fan, _unused = fan_out(boxes.astype(jnp.float32), -1)
+    sums = jnp.dot(fan, post, preferred_element_type=jnp.float32)
+    both = sums[:, :half]
+    for p in range(1, COARSE // 2):
+        both = both + roll_rows(sums[:, p * half : (p + 1) * half], -2 * p * SHIFT * FINE)
+    whole = both + pltpu.roll(roll_rows(both, -SHIFT * FINE), half // 2, 1)
+    return whole.T
+
+
+def plain_sums_kernel(width, boxes_ref, post_ref, mass_ref, out_ref):
+    turned = turned_sums(boxes_ref[...], post_ref[...])
+    classes = out_ref.shape[2]
+    mass = jnp.broadcast_to(mass_ref[...], (128, 128)).T
+    for h in range(2):
+        rows = turned[h * classes : (h + 1) * classes]
+        tail = mass[h * classes : (h + 1) * classes, : out_ref.shape[3] - width]
+        for j in range(STEP // width):
+            out_ref[j, h, :, :width] = rows[:, j * width : (j + 1) * width]
+            out_ref[j, h, :, width:] = tail
+
+
+def plain_sums(boxes, post, mass, classes, peers):
+    width = CYCLES // peers * ANGLES
     padded = (width + 1 + 127) // 128 * 128
-    owned = boxes.shape[0]
-    classes = refs.shape[0]
-    half = 2 * classes
-    if width >= STEP:
-        per = width // STEP
-        out_spec = pl.BlockSpec((1, 2, classes // 2, padded), lambda p, i: (p * (i // per), 0, 0, 0))
-    else:
-        out_spec = pl.BlockSpec(
-            (STEP // width, 2, classes // 2, padded), lambda p, i: (p * i, 0, 0, 0)
-        )
-    hold = lambda p, i: i * (1 - p) + (STEPS - 1) * p
     return pl.pallas_call(
-        functools.partial(kernel, cycles_dev),
-        grid=(2, STEPS),
+        functools.partial(plain_sums_kernel, width),
+        grid=(STEPS,),
         in_specs=[
-            pl.BlockSpec((owned, STEP), lambda p, i: (0, i)),
-            pl.BlockSpec((classes, STEP), lambda p, i: (0, hold(p, i))),
-            pl.BlockSpec((1, owned, STEP_CYCLES), lambda p, i: (hold(p, i), 0, 0)),
-            pl.BlockSpec(aux.shape, lambda p, i: (0, 0)),
-            pl.BlockSpec((1, half), lambda p, i: (0, 0)),
-        ],
-        out_specs=[out_spec, pl.BlockSpec((owned, 1), lambda p, i: (0, 0))],
+            pl.BlockSpec((boxes.shape[0], STEP), lambda i: (0, i)),
+            pl.BlockSpec(post.shape, lambda i: (0, 0)),
+            pl.BlockSpec(mass.shape, lambda i: (0, 0)),
+        ],
+        out_specs=pl.BlockSpec((STEP // width, 2, classes, padded), lambda i: (i, 0, 0, 0)),
+        out_shape=jax.ShapeDtypeStruct((peers, 2, classes, padded), jnp.float32),
+    )(boxes, post, mass)
+
+
+def scores(boxes, refs, wts, aux, strength):
+    owned, classes, half = boxes.shape[0], refs.shape[0], strength.shape[1]
+    whole = lambda shape: pl.BlockSpec(shape, lambda i: (0, 0))
+    post = (FINE * owned, COARSE * classes)
+    return pl.pallas_call(
+        score_kernel,
+        grid=(STEPS,),
+        in_specs=[
+            pl.BlockSpec((owned, STEP), lambda i: (0, i)),
+            pl.BlockSpec((classes, STEP), lambda i: (0, i)),
+            pl.BlockSpec((1, owned, STEP_CYCLES), lambda i: (i, 0, 0)),
+            whole(aux.shape),
+            whole((1, half)),
+        ],
+        out_specs=[whole(post), whole((1, half)), whole((owned, 1))],
         out_shape=[
-            jax.ShapeDtypeStruct((peers, 2, classes // 2, padded), jnp.float32),
+            jax.ShapeDtypeStruct(post, jnp.bfloat16),
+            jax.ShapeDtypeStruct((1, half), jnp.float32),
             jax.ShapeDtypeStruct((owned, 1), jnp.float32),
         ],
         scratch_shapes=[
             pltpu.VMEM((COARSE, 2 * owned, FINE * classes), jnp.float32),
             pltpu.VMEM((owned, half), jnp.float32),
-            pltpu.VMEM((FINE * owned, COARSE * classes), jnp.bfloat16),
-            pltpu.VMEM((half, half), jnp.float32),
         ],
         compiler_params=pltpu.CompilerParams(
-            dimension_semantics=("arbitrary", "arbitrary"), vmem_limit_bytes=40 * 1024 * 1024
+            dimension_semantics=("arbitrary",), vmem_limit_bytes=40 * 1024 * 1024
         ),
     )(boxes, refs, wts, aux, strength)
 
@@ -326,6 +327,111 @@
             collective_id=1, has_side_effects=True, vmem_limit_bytes=48 * 1024 * 1024
         ),
     )(parts.reshape(depth, 2, 2, classes, width))
+
+
+def sums_kernel(peers, boxes, post, mass, refs, out, pair_out, pair_in, keep, side_out, side_in,
+                line_in, mass_in, column, pair_send, pair_recv, side_send, side_recv, line_send,
+                line_recv, mass_send, mass_recv):
+    mine, core = lax.axis_index("particle"), lax.axis_index("classes")
+    depth, width, classes = peers // 2, out.shape[1], out.shape[0]
+    level, side = mine // 2, lax.rem(mine, 2)
+    place = mine * 2 + core
+    partner = {"classes": 1 - core}
+    across = {"particle": level * 2 + 1 - side}
+    everyone = []
+    for e in range(1, 2 * peers):
+        there = lax.rem(place + e, 2 * peers)
+        everyone.append({"particle": there // 2, "classes": lax.rem(there, 2)})
+    greet(everyone)
+    started, masses = [], []
+
+    def send(src, dst, sends, recvs, device):
+        copy = pltpu.make_async_remote_copy(
+            src_ref=src, dst_ref=dst, send_sem=sends, recv_sem=recvs, device_id=device,
+            device_id_type=MESH,
+        )
+        copy.start()
+        started.append(copy)
+        return copy
+
+    for e, device in enumerate(everyone):
+        masses.append(
+            send(mass, mass_in.at[e], mass_send.at[e], mass_recv.at[e], device)
+        )
+    turns = list(range(1, depth)) + [0]
+    blocks = [(i, d, True) for i, d in enumerate(turns)] + [(i, d, False) for i, d in enumerate(turns)]
+    pair, cross, lines = [], [], []
+
+    def advance(n):
+        i, d, away = blocks[n]
+        pair[n].wait_recv()
+        if away:
+            side_out[i] = keep[n] + pair_in[n]
+            cross.append(
+                send(side_out.at[i], side_in.at[i], side_send.at[i], side_recv.at[i], across)
+            )
+            return
+        cross[i].wait_recv()
+        keep[n] = keep[n] + pair_in[n] + side_in[i]
+        if d > 0:
+            there = {"particle": lax.rem(level + d, depth) * 2 + side}
+            lines.append(
+                send(keep.at[n], line_in.at[i], line_send.at[i], line_recv.at[i], there)
+            )
+
+    for n, (i, d, away) in enumerate(blocks):
+        shard = lax.rem(level + d, depth) * 2 + (1 - side if away else side)
+
+        @pl.loop(0, width // STEP)
+        def _(part):
+            source = pl.multiple_of(shard * width + part * STEP, 128)
+            target = pl.multiple_of(part * STEP, 128)
+            turned = turned_sums(boxes[:, pl.ds(source, STEP)], post[...])
+            low, high = turned[:classes], turned[classes : 2 * classes]
+            keep[n, :, pl.ds(target, STEP)] = jnp.where(core == 0, low, high)
+            pair_out[n, :, pl.ds(target, STEP)] = jnp.where(core == 0, high, low)
+
+        pair.append(send(pair_out.at[n], pair_in.at[n], pair_send.at[n], pair_recv.at[n], partner))
+        if n > 0:
+            advance(n - 1)
+    advance(len(blocks) - 1)
+    weight = mass[...]
+    for e, copy in enumerate(masses):
+        copy.wait_recv()
+        weight = weight + mass_in[e]
+    column[...] = jnp.broadcast_to(weight, column.shape).T
+    scale = column[pl.ds(pl.multiple_of(core * classes, 8), classes), :]
+    total = keep[len(blocks) - 1]
+    for i in range(depth - 1):
+        lines[i].wait_recv()
+        total = total + line_in[i]
+    base = refs[:, pl.ds(pl.multiple_of(mine * width, 128), width)].astype(jnp.float32)
+    out[...] = (total + base) / (scale[:, 0:1] + 1.0)
+    for copy in started:
+        copy.wait_send()
+
+
+def fused_sums(boxes, post, mass, refs, peers):
+    classes, width, depth = refs.shape[0], CYCLES // peers * ANGLES, peers // 2
+    room = lambda count: pltpu.VMEM((count, classes, width), jnp.float32)
+    sems = lambda count: pltpu.SemaphoreType.DMA((count,))
+    others = 2 * peers - 1
+    return pl.pallas_call(
+        functools.partial(sums_kernel, peers),
+        in_specs=[pl.BlockSpec(memory_space=pltpu.VMEM)] * 4,
+        out_specs=pl.BlockSpec(memory_space=pltpu.VMEM),
+        out_shape=jax.ShapeDtypeStruct((classes, width), jnp.float32),
+        scratch_shapes=[
+            room(peers), room(peers), room(peers), room(depth), room(depth), room(depth - 1),
+            pltpu.VMEM((others,) + mass.shape, jnp.float32),
+            pltpu.VMEM((mass.shape[1], mass.shape[1]), jnp.float32),
+            sems(peers), sems(peers), sems(depth), sems(depth), sems(depth - 1), sems(depth - 1),
+            sems(others), sems(others),
+        ],
+        compiler_params=pltpu.CompilerParams(
+            collective_id=2, has_side_effects=True, vmem_limit_bytes=48 * 1024 * 1024
+        ),
+    )(boxes, post, mass, refs)
 
 
 def on_device(boxes, counts, destinations, prior_rot, references, cycle_weights, prior_strength):
@@ -354,14 +460,17 @@
     gap = TWO_PI * (turn_ids[None, :] - prior_rot[:, None].astype(jnp.float32)) / ROTATIONS
     aux = jnp.concatenate([jnp.cos(gap), live[:, None], jnp.sum(wts, axis=1)[:, None]], axis=1)
     wts = jnp.transpose(wts.reshape(owned, STEPS, STEP_CYCLES), (1, 0, 2))
-    parts, evidence = class_terms(
-        boxes, refs, wts, aux, jnp.concatenate([strength, strength], axis=1), peers
+    post, mass, evidence = scores(
+        boxes, refs, wts, aux, jnp.concatenate([strength, strength], axis=1)
     )
-    sums = scattered(parts)
-    own_refs = lax.dynamic_slice_in_dim(references, cycle_index * width, width, 1)
-    new_references = (sums[:, :width] + own_refs.astype(jnp.float32)) / (
-        sums[:, width : width + 1] + 1.0
-    )
+    if width % STEP == 0:
+        new_references = fused_sums(boxes, post, mass, references, peers)
+    else:
+        sums = scattered(plain_sums(boxes, post, mass, classes_dev, peers))
+        own_refs = lax.dynamic_slice_in_dim(references, cycle_index * width, width, 1)
+        new_references = (sums[:, :width] + own_refs.astype(jnp.float32)) / (
+            sums[:, width : width + 1] + 1.0
+        )
     return new_references.reshape(classes_dev, cycles_dev, ANGLES), evidence[:, 0]
 
 

time: 75.4 us -> 64.6 us (0.86)
  Pallas kernels: 63.1 us -> 53.5 us
  other arithmetic: 6.48 us -> 5.38 us
    pallas_call x2, Pallas kernels: 52.5 us -> 42.9 us  [the longest x1 31.3 us: fused_sums(): pl.pallas_call(functools.partial(sums_kernel, peers), in_specs=[pl.BlockS...]
    div x1 -> x0, other arithmetic: 0.99 us -> none  [on_device(): (sums[:, :width] + own_refs.astype(jnp.float32)) / (sums[:, width:width +...]
where the time goes in v2:
time: 64.6 us; the launch traced here: 64.4 us
  Pallas kernels  53.5 us (83%)
  other arithmetic  5.38 us (8%)
  local copies, waits for them, and re-layouts  4.04 us (6%)
  between operations  1.49 us (2%)
    pallas_call x1, Pallas kernels, fused_sums(): pl.pallas_call(functools.partial(sums_kernel, peers), in_specs=[pl.BlockS...  31.3 us
    pallas_call x1, Pallas kernels, scores(): pl.pallas_call(score_kernel, grid=(STEPS,), in_specs=[pl.BlockSpec((owned...  11.5 us
    pallas_call x1, Pallas kernels, gathered(): pl.pallas_call(functools.partial(gather_kernel, peers), in_specs=[pl.Bloc...  10.6 us
    unnamed x6, local copies, waits for them, and re-layouts  1.41 us

profile of v2, /device:TPU:0, one launch (start us, length us, event | category | flops | bytes accessed | tf_op | source)
XLA Modules:
  0.0 64.4 jit_solution(7582413881461455401)
XLA Ops:
  0.6 0.0 copy-start
  1.4 0.7 %convert_element_type.16 = f32[64]{0:T(128)S(1)} convert(s32[64]{0:T(128)} %param.10) | non-fusion elementwise | flops 64 | bytes 512 | tf_op jit(solution)/shard_map/convert_element_type | solution.py:460
  2.1 1.3 %fusion.2.row_ref = f32[1,128]{1,0:T(1,128)} fusion(f32[32]{0:T(128)} %param.13, f32[64]{0:T(128)} %bitcast.19), kind=kLoop, calls=%fused_computation.13 | loop fusion | flops 512 | bytes 896 | tf_op jit(solution)/shard_map/broadcast_in_dim | solution.py:446
  3.3 0.7 %iota_compare_fusion.1 = pred[64,8]{1,0:T(8,128)(4,1)S(1)} fusion(s32[64]{0:T(128)} %param.9), kind=kLoop, calls=%fused_computation.5 | loop fusion | flops 512 | bytes 768 | tf_op jit(solution)/shard_map/eq | solution.py:456
  4.1 0.2 multiply_cosine_fusion
  4.3 10.6 %shard_map.86 = (bf16[2,32,12288]{2,1,0:T(8,128)(2,1)}, f32[9,1,128]{2,1,0:T(1,128)}) custom-call(bf16[32,12288]{1,0:T(8,128)(2,1)} %refs.1, f32[1,128]{1,0:T(1,128)} %fusion.2.row_ref), custom_call_target="tpu_custom_call" | custom-call | tf_op jit(solution)/shard_map/pallas_call | solution.py:239
  14.9 0.7 %slice_bitcast_fusion = f32[1,32]{1,0:T(1,128)S(1)} fusion(f32[9,1,128]{2,1,0:T(1,128)} %get-tuple-element.8), kind=kLoop, calls=%fused_computation.12 | loop fusion | bytes 256 | tf_op jit(solution)/shard_map/concatenate | solution.py:453
  15.6 0.7 %slice.6 = f32[8,1,64]{2,1,0:T(1,128)S(1)} slice(f32[9,1,128]{2,1,0:T(1,128)} %get-tuple-element.8), slice={[0:8], [0:1], [0:64]} | slice | bytes 4096 | tf_op jit(solution)/shard_map/slice | solution.py:449
  16.3 0.8 %broadcast_select_fusion = f32[1,64]{1,0:T(1,128)S(1)} fusion(pred[]{:T(512)S(6)} %eq.23, f32[1,32]{1,0:T(1,128)S(1)} %slice_bitcast_fusion, f32[1,32]{1,0:T(1,128)} %bitcast.18), kind=kLoop, calls=%fused_computation.9 | loop fusion | flops 192 | bytes 513 | tf_op jit(solution)/shard_map/jit(_where)/select_n | solution.py:451
  17.1 0.1 pad_maximum_fusion.1.str_ref
  17.2 0.9 %select_reduce_fusion = (f32[64]{0:T(128)S(1)}, f32[64,64]{1,0:T(8,128)S(1)}) fusion(f32[8,64]{1,0:T(8,128)S(1)} %bitcast.16, pred[64,8]{1,0:T(8,128)(4,1)S(1)} %iota_compare_fusion.1), kind=kLoop, calls=%fused_computation | loop fusion | flops 94144 | bytes 19200 | tf_op jit(solution)/shard_map/reduce_sum | solution.py:461
  18.1 0.1 copy.14
  18.2 0.1 pad_maximum_fusion.aux_ref
  18.3 0.1 copy.12
  18.4 0.2 copy.13
  18.6 0.0 copy-done
  18.7 0.0 copy-start.2
  18.7 1.4 %copy-done.2 = bf16[2,32,12288]{2,1,0:T(8,128)(2,1)S(1)} copy-done((bf16[2,32,12288]{2,1,0:T(8,128)(2,1)S(1)}, bf16[2,32,12288]{2,1,0:T(8,128)(2,1)}, u32[]{:S(2)}) %copy-start.2) | copy-done | bytes 1572888
  20.1 0.0 copy-start.1
  20.1 11.5 %shard_map.87 = (bf16[256,384]{1,0:T(8,128)(2,1)S(1)}, f32[1,128]{1,0:T(1,128)S(1)}, f32[64,1]{1,0:T(8,128)S(1)}) custom-call(bf16[64,12288]{1,0:T(8,128)(2,1)S(1)} %copy-done, bf16[64,12288]{1,0:T(8,128)(2,1)S(1)} %bitcast.14, f32[16,64,4]{2,1,0:T(8,128)S(1)} %bitcast.13, f32[64,26]{1,0:T(8,128)S(1)} %pad_maximum_fusion.aux_ref, ...), custom_call_target="tpu_custom_call" | custom-call | tf_op jit(solution)/shard_map/pallas_call | solution.py:167
  31.6 0.0 copy-done.1
  31.6 31.3 %shard_map.88 = f32[32,1536]{1,0:T(8,128)S(1)} custom-call(bf16[64,12288]{1,0:T(8,128)(2,1)S(1)} %copy-done, bf16[256,384]{1,0:T(8,128)(2,1)S(1)} %get-tuple-element.9.post, f32[1,128]{1,0:T(1,128)S(1)} %get-tuple-element.10.mass, bf16[32,12288]{1,0:T(8,128)(2,1)S(1)} %copy-done.1), custom_call_target="tpu_custom_call" | custom-call | tf_op jit(solution)/shard_map/pallas_call | solution.py:419
  62.9 0.6 reduce.1
  63.6 0.8 %reshape.107 = f32[32,8,192]{2,1,0:T(8,128)} reshape(f32[32,1536]{1,0:T(8,128)S(1)} %shard_map.88) | data formatting | bytes 393216 | tf_op jit(solution)/shard_map/reshape | solution.py:474
  (1 shorter events, 0.0 us)
Async XLA Ops:
  0.6 18.0 %copy-start = (bf16[64,12288]{1,0:T(8,128)(2,1)S(1)}, bf16[64,12288]{1,0:T(8,128)(2,1)}, u32[]{:S(2)}) copy-start(bf16[64,12288]{1,0:T(8,128)(2,1)} %boxes.1) | copy-start | bytes 4718596
  18.7 1.4 %copy-start.2 = (bf16[2,32,12288]{2,1,0:T(8,128)(2,1)S(1)}, bf16[2,32,12288]{2,1,0:T(8,128)(2,1)}, u32[]{:S(2)}) copy-start(bf16[2,32,12288]{2,1,0:T(8,128)(2,1)} %get-tuple-element.7) | copy-start | bytes 4718596
  20.1 11.6 %copy-start.1 = (bf16[32,12288]{1,0:T(8,128)(2,1)S(1)}, bf16[32,12288]{1,0:T(8,128)(2,1)}, u32[]{:S(2)}) copy-start(bf16[32,12288]{1,0:T(8,128)(2,1)} %refs.1) | copy-start | bytes 2359300

commit v3 on v2

--- a/solution.py
+++ b/solution.py
@@ -358,7 +358,7 @@
         masses.append(
             send(mass, mass_in.at[e], mass_send.at[e], mass_recv.at[e], device)
         )
-    turns = list(range(1, depth)) + [0]
+    turns = sorted(range(1, depth), key=lambda d: -min(d, depth - d)) + [0]
     blocks = [(i, d, True) for i, d in enumerate(turns)] + [(i, d, False) for i, d in enumerate(turns)]
     pair, cross, lines = [], [], []
 

time: 64.6 us -> 64.8 us (level)
  no operation moved by 1% of the time
where the time goes in v3:
time: 64.8 us; the launch traced here: 64.5 us
  Pallas kernels  53.6 us (83%)
  other arithmetic  5.38 us (8%)
  local copies, waits for them, and re-layouts  4.04 us (6%)
  between operations  1.49 us (2%)
    pallas_call x1, Pallas kernels, fused_sums(): pl.pallas_call(functools.partial(sums_kernel, peers), in_specs=[pl.BlockS...  31.5 us
    pallas_call x1, Pallas kernels, scores(): pl.pallas_call(score_kernel, grid=(STEPS,), in_specs=[pl.BlockSpec((owned...  11.5 us
    pallas_call x1, Pallas kernels, gathered(): pl.pallas_call(functools.partial(gather_kernel, peers), in_specs=[pl.Bloc...  10.6 us
    unnamed x6, local copies, waits for them, and re-layouts  1.41 us

profile of v3, /device:TPU:0, one launch (start us, length us, event | category | flops | bytes accessed | tf_op | source)
XLA Modules:
  0.0 64.5 jit_solution(15273730115672602688)
XLA Ops:
  0.6 0.0 copy-start
  1.4 0.7 %convert_element_type.16 = f32[64]{0:T(128)S(1)} convert(s32[64]{0:T(128)} %param.10) | non-fusion elementwise | flops 64 | bytes 512 | tf_op jit(solution)/shard_map/convert_element_type | solution.py:460
  2.1 1.3 %fusion.2.row_ref = f32[1,128]{1,0:T(1,128)} fusion(f32[32]{0:T(128)} %param.13, f32[64]{0:T(128)} %bitcast.19), kind=kLoop, calls=%fused_computation.13 | loop fusion | flops 512 | bytes 896 | tf_op jit(solution)/shard_map/broadcast_in_dim | solution.py:446
  3.3 0.7 %iota_compare_fusion.1 = pred[64,8]{1,0:T(8,128)(4,1)S(1)} fusion(s32[64]{0:T(128)} %param.9), kind=kLoop, calls=%fused_computation.5 | loop fusion | flops 512 | bytes 768 | tf_op jit(solution)/shard_map/eq | solution.py:456
  4.1 0.2 multiply_cosine_fusion
  4.3 10.6 %shard_map.86 = (bf16[2,32,12288]{2,1,0:T(8,128)(2,1)}, f32[9,1,128]{2,1,0:T(1,128)}) custom-call(bf16[32,12288]{1,0:T(8,128)(2,1)} %refs.1, f32[1,128]{1,0:T(1,128)} %fusion.2.row_ref), custom_call_target="tpu_custom_call" | custom-call | tf_op jit(solution)/shard_map/pallas_call | solution.py:239
  14.9 0.7 %slice_bitcast_fusion = f32[1,32]{1,0:T(1,128)S(1)} fusion(f32[9,1,128]{2,1,0:T(1,128)} %get-tuple-element.8), kind=kLoop, calls=%fused_computation.12 | loop fusion | bytes 256 | tf_op jit(solution)/shard_map/concatenate | solution.py:453
  15.6 0.7 %slice.6 = f32[8,1,64]{2,1,0:T(1,128)S(1)} slice(f32[9,1,128]{2,1,0:T(1,128)} %get-tuple-element.8), slice={[0:8], [0:1], [0:64]} | slice | bytes 4096 | tf_op jit(solution)/shard_map/slice | solution.py:449
  16.3 0.8 %broadcast_select_fusion = f32[1,64]{1,0:T(1,128)S(1)} fusion(pred[]{:T(512)S(6)} %eq.23, f32[1,32]{1,0:T(1,128)S(1)} %slice_bitcast_fusion, f32[1,32]{1,0:T(1,128)} %bitcast.18), kind=kLoop, calls=%fused_computation.9 | loop fusion | flops 192 | bytes 513 | tf_op jit(solution)/shard_map/jit(_where)/select_n | solution.py:451
  17.1 0.1 pad_maximum_fusion.1.str_ref
  17.2 0.9 %select_reduce_fusion = (f32[64]{0:T(128)S(1)}, f32[64,64]{1,0:T(8,128)S(1)}) fusion(f32[8,64]{1,0:T(8,128)S(1)} %bitcast.16, pred[64,8]{1,0:T(8,128)(4,1)S(1)} %iota_compare_fusion.1), kind=kLoop, calls=%fused_computation | loop fusion | flops 94144 | bytes 19200 | tf_op jit(solution)/shard_map/reduce_sum | solution.py:461
  18.1 0.1 copy.14
  18.2 0.1 pad_maximum_fusion.aux_ref
  18.3 0.1 copy.12
  18.4 0.2 copy.13
  18.6 0.0 copy-done
  18.7 0.0 copy-start.2
  18.7 1.4 %copy-done.2 = bf16[2,32,12288]{2,1,0:T(8,128)(2,1)S(1)} copy-done((bf16[2,32,12288]{2,1,0:T(8,128)(2,1)S(1)}, bf16[2,32,12288]{2,1,0:T(8,128)(2,1)}, u32[]{:S(2)}) %copy-start.2) | copy-done | bytes 1572888
  20.1 0.0 copy-start.1
  20.1 11.5 %shard_map.87 = (bf16[256,384]{1,0:T(8,128)(2,1)S(1)}, f32[1,128]{1,0:T(1,128)S(1)}, f32[64,1]{1,0:T(8,128)S(1)}) custom-call(bf16[64,12288]{1,0:T(8,128)(2,1)S(1)} %copy-done, bf16[64,12288]{1,0:T(8,128)(2,1)S(1)} %bitcast.14, f32[16,64,4]{2,1,0:T(8,128)S(1)} %bitcast.13, f32[64,26]{1,0:T(8,128)S(1)} %pad_maximum_fusion.aux_ref, ...), custom_call_target="tpu_custom_call" | custom-call | tf_op jit(solution)/shard_map/pallas_call | solution.py:167
  31.6 0.0 copy-done.1
  31.6 31.5 %shard_map.88 = f32[32,1536]{1,0:T(8,128)S(1)} custom-call(bf16[64,12288]{1,0:T(8,128)(2,1)S(1)} %copy-done, bf16[256,384]{1,0:T(8,128)(2,1)S(1)} %get-tuple-element.9.post, f32[1,128]{1,0:T(1,128)S(1)} %get-tuple-element.10.mass, bf16[32,12288]{1,0:T(8,128)(2,1)S(1)} %copy-done.1), custom_call_target="tpu_custom_call" | custom-call | tf_op jit(solution)/shard_map/pallas_call | solution.py:419
  63.1 0.6 reduce.1
  63.7 0.8 %reshape.107 = f32[32,8,192]{2,1,0:T(8,128)} reshape(f32[32,1536]{1,0:T(8,128)S(1)} %shard_map.88) | data formatting | bytes 393216 | tf_op jit(solution)/shard_map/reshape | solution.py:474
  (1 shorter events, 0.0 us)
Async XLA Ops:
  0.6 18.0 %copy-start = (bf16[64,12288]{1,0:T(8,128)(2,1)S(1)}, bf16[64,12288]{1,0:T(8,128)(2,1)}, u32[]{:S(2)}) copy-start(bf16[64,12288]{1,0:T(8,128)(2,1)} %boxes.1) | copy-start | bytes 4718596
  18.7 1.4 %copy-start.2 = (bf16[2,32,12288]{2,1,0:T(8,128)(2,1)S(1)}, bf16[2,32,12288]{2,1,0:T(8,128)(2,1)}, u32[]{:S(2)}) copy-start(bf16[2,32,12288]{2,1,0:T(8,128)(2,1)} %get-tuple-element.7) | copy-start | bytes 4718596
  20.1 11.6 %copy-start.1 = (bf16[32,12288]{1,0:T(8,128)(2,1)S(1)}, bf16[32,12288]{1,0:T(8,128)(2,1)}, u32[]{:S(2)}) copy-start(bf16[32,12288]{1,0:T(8,128)(2,1)} %refs.1) | copy-start | bytes 2359300
